TPU v7x, 32 devices: a whole 2x2x4 slice. The times are simulated.
32 devices in a mesh: groups: 2 (over y), row: 8 (over z, x), col: 2 (over core).
Axes of the slice: x: 2, y: 2, z: 4, core: 2. Of those that a mesh axis runs over, the one named last changes fastest.
Arguments:
- embeddings: bfloat16 [128, 16, 1280], P(('groups', 'row'), 'col'), parts along dimension 0, may hold values from -6 to 52
- pos_embed: bfloat16 [256, 1280], replicated, may hold values from -3 to 3
- ln_gain: float32 [1280], replicated, may hold values from 0.6 to 9
- ln_bias: float32 [1280], replicated, may hold values from -1.5 to 1.5
- w_qkv: bfloat16 [1280, 1920], P(('row', 'col')), may hold values from -0.25155765 to 0.25155765
- b_qkv: float32 [1920], replicated, may hold values from -1.5 to 1.5
- w_out: bfloat16 [1280, 640], P(('row', 'col')), may hold values from -0.25 to 0.25
- b_out: float32 [1280], replicated, may hold values from -1.5 to 1.5
- valid: int32 [16, 2, 256], P(('groups', 'row'), 'col'), parts along dimension 0, may hold values from 0 to 196
Outputs:
- merged: bfloat16 [128, 16, 1280], P(('groups', 'row'), 'col'), parts along dimension 0
There are 2 independent parts, one for each index of `groups`. A program takes and returns all parts, laid end to end along the dimension named above; an argument that names none is the same for every part. Nothing has to cross between parts.
All inputs are finite; a program needn't handle non-finite values.
Results may differ from a plain program's by a relative error of at most 0.0098.
Values may be sent and summed in bfloat16 or wider, within the bound.
A program may use at most 64 MiB of HBM per device.

v0:
```python
import jax
import jax.numpy as jnp
from jax import lax
from jax.sharding import PartitionSpec as P

HEADS = 8


EPSILON = 1e-06
SPREAD = 4.0
FLOOR = 0.25


def shifted(value, axis, steps):
    count = lax.axis_size(axis)
    initial, last = (max(0, -steps), min(count, count - steps))
    return lax.ppermute(value, axis, [(source, source + steps) for source in range(initial, last)])


def extended(block, sides, width):
    for axis, dim in sides:
        count = lax.axis_size(axis)
        forward = [(i, i + 1) for i in range(count - 1)]
        backward = [(target, source) for source, target in forward]
        low = lax.ppermute(
            lax.slice_in_dim(block, block.shape[dim] - width, None, axis=dim), axis, forward
        )
        high = lax.ppermute(lax.slice_in_dim(block, 0, width, axis=dim), axis, backward)
        block = jnp.concatenate([low, block, high], axis=dim)
    return block


def layer_norm(inputs, ln_gain, ln_bias):
    centred = inputs - jnp.mean(inputs, axis=-1, keepdims=True)
    variance = jnp.mean(centred * centred, axis=-1, keepdims=True)
    return centred * lax.rsqrt(variance + EPSILON) * ln_gain + ln_bias


def gauss_table(win):
    offsets = jnp.arange(win, dtype=jnp.float32) - (win - 1) / 2.0
    squared = offsets[:, None] * offsets[:, None] + offsets[None, :] * offsets[None, :]
    return jnp.exp(-squared / (2.0 * SPREAD * SPREAD))


def attend(projected):
    rows_count = projected.shape[0]
    width = projected.shape[1] // 3
    head_size = width // HEADS
    queries = projected[:, :width].reshape(rows_count, HEADS, head_size)
    keys = projected[:, width : 2 * width].reshape(rows_count, HEADS, head_size)
    values = projected[:, 2 * width :].reshape(rows_count, HEADS, head_size)
    scores = jnp.einsum(
        "qhd,khd->hqk", queries, keys, preferred_element_type=jnp.float32
    ) * head_size ** (-0.5)
    highest = jnp.max(scores, axis=-1, keepdims=True)
    expon = jnp.exp(scores - highest)
    probs = (expon / jnp.sum(expon, axis=-1, keepdims=True)).astype(jnp.bfloat16)
    mixed = jnp.einsum("hqk,khd->qhd", probs, values, preferred_element_type=jnp.float32)
    return mixed.astype(jnp.bfloat16).reshape(rows_count, width)


def fold_rows(numerator, denominator, rim):
    from_next = (
        shifted(numerator[:rim].astype(jnp.bfloat16), "row", -1).astype(jnp.float32),
        shifted(denominator[:rim].astype(jnp.bfloat16), "row", -1).astype(jnp.float32),
    )
    from_prev = (
        shifted(numerator[-rim:].astype(jnp.bfloat16), "row", 1).astype(jnp.float32),
        shifted(denominator[-rim:].astype(jnp.bfloat16), "row", 1).astype(jnp.float32),
    )
    middle_num = numerator[rim:-rim]
    middle_den = denominator[rim:-rim]
    middle_num = middle_num.at[:rim].add(from_prev[0]).at[-rim:].add(from_next[0])
    middle_den = middle_den.at[:rim].add(from_prev[1]).at[-rim:].add(from_next[1])
    return (middle_num, middle_den)


def fold_cols(numerator, denominator, rim):
    from_next = (
        shifted(numerator[:, :rim].astype(jnp.bfloat16), "col", -1).astype(jnp.float32),
        shifted(denominator[:, :rim].astype(jnp.bfloat16), "col", -1).astype(jnp.float32),
    )
    from_prev = (
        shifted(numerator[:, -rim:].astype(jnp.bfloat16), "col", 1).astype(jnp.float32),
        shifted(denominator[:, -rim:].astype(jnp.bfloat16), "col", 1).astype(jnp.float32),
    )
    middle_num = numerator[:, rim:-rim] + jnp.concatenate([from_prev[0], from_next[0]], axis=1)
    middle_den = denominator[:, rim:-rim] + jnp.concatenate([from_prev[1], from_next[1]], axis=1)
    return (middle_num, middle_den)


def body(embeddings, pos_embed, ln_gain, ln_bias, w_qkv, b_qkv, w_out, b_out, valid):
    tile = embeddings.shape[1]
    tile_rows = embeddings.shape[0] // tile
    rim = tile // 2
    win = tile + 2 * rim
    rows_count = win * win
    width_model = embeddings.shape[2]
    window = extended(embeddings, (("row", 0), ("col", 1)), rim)
    stacked = jnp.stack([window], axis=0)
    inputs = stacked.reshape(tile_rows, rows_count, width_model).astype(
        jnp.float32
    ) + pos_embed.astype(jnp.float32)
    inputs = inputs.reshape(tile_rows * rows_count, width_model)
    normed = layer_norm(inputs, ln_gain, ln_bias).astype(jnp.bfloat16)
    projected = jnp.dot(
        normed,
        lax.all_gather(w_qkv, ("row", "col"), axis=0, tiled=True),
        preferred_element_type=jnp.float32,
    )
    projected = (
        (projected + b_qkv).astype(jnp.bfloat16).reshape(tile_rows, rows_count, w_qkv.shape[1])
    )
    attended = jax.vmap(attend)(projected).reshape(tile_rows * rows_count, -1)
    projected_out = lax.dot_general(
        attended,
        lax.all_gather(w_out, ("row", "col"), axis=0, tiled=True),
        (((1,), (1,)), ((), ())),
        preferred_element_type=jnp.float32,
    )
    hidden = inputs + projected_out + b_out
    gauss = gauss_table(win).reshape(1, rows_count)
    weight = gauss * valid.reshape(tile_rows, rows_count).astype(jnp.float32) / 196.0
    contrib = (weight.reshape(tile_rows * rows_count, 1) * hidden).reshape(
        tile_rows, win, win, width_model
    )
    weight_grid = weight.reshape(tile_rows, win, win)
    numerator = jnp.zeros((tile_rows * tile + 2 * rim, win, width_model), jnp.float32)
    denominator = jnp.zeros((tile_rows * tile + 2 * rim, win), jnp.float32)
    numerator = numerator.at[0:win].add(contrib[0])
    denominator = denominator.at[0:win].add(weight_grid[0])
    numerator, denominator = fold_rows(numerator, denominator, rim)
    numerator, denominator = fold_cols(numerator, denominator, rim)
    return (numerator / jnp.maximum(denominator, FLOOR)[:, :, None]).astype(jnp.bfloat16)


def solution(mesh):
    placed = (
        P(("groups", "row"), "col", None),
        P(),
        P(),
        P(),
        P(("row", "col"), None),
        P(),
        P(("row", "col"), None),
        P(),
        P(("groups", "row"), "col", None),
    )
    return jax.shard_map(
        body,
        mesh=mesh,
        in_specs=placed,
        out_specs=P(("groups", "row"), "col", None),
        check_vma=False,
    )
```

profile of v0, /device:TPU:0, one launch (start us, length us, event | category | flops | bytes accessed | tf_op | source)
XLA Modules:
  0.0 136.9 jit_solution(5850899575125565786)
XLA Ops:
  7.3 0.9 fusion.25
  8.2 4.9 %collective-permute-start = (bf16[4,8,1280]{2,1,0:T(8,128)(2,1)S(1)}, bf16[4,8,1280]{2,1,0:T(8,128)(2,1)S(1)}, u32[]{:S(2)}, u32[]{:S(2)}) collective-permute-start(bf16[4,8,1280]{2,1,0:T(8,128)(2,1)S(1)} %get-tuple-element.105), channel_id=1, source_target_pairs={{0,2},{2,4},{4,6},{6,8},{8,10},{10,12},{12,14},{1,3},{3,5},{5,7},{... | collective-permute-start | bytes 245768 | tf_op jit(solution)/shard_map/ppermute | solution.py:25
  13.1 1.3 collective-permute-start.1
  15.3 4.5 %collective-permute-start.8 = (bf16[4,16]{1,0:T(4,128)(2,1)S(1)}, bf16[4,16]{1,0:T(4,128)(2,1)S(1)}, u32[]{:S(2)}, u32[]{:S(2)}) collective-permute-start(bf16[4,16]{1,0:T(4,128)(2,1)S(1)} %get-tuple-element.107), channel_id=1, source_target_pairs={{0,2},{2,4},{4,6},{6,8},{8,10},{10,12},{12,14},{1,3},{3,5},{5,7},{... | collective-permute-start | bytes 392 | tf_op jit(solution)/shard_map/ppermute | solution.py:17
  19.9 1.3 collective-permute-start.9
  22.1 1.0 constant_dynamic-update-slice_fusion.1
  23.2 1.3 collective-permute-start.2
  24.6 1.3 collective-permute-start.3
  25.9 1.9 %collective-permute-done.3 = bf16[16,4,1280]{2,1,0:T(4,128)(2,1)S(1)} collective-permute-done((bf16[16,4,1280]{2,1,0:T(4,128)(2,1)S(1)}, bf16[16,4,1280]{2,1,0:T(4,128)(2,1)S(1)}, u32[]{:S(2)}, u32[]{:S(2)}) %collective-permute-start.3) | collective-permute-done | bytes 163872 | tf_op jit(solution)/shard_map/ppermute | solution.py:28
  28.9 37.5 %all-gather.3.cloned.1.call-done = bf16[1280,1920]{1,0:T(8,128)(2,1)} async-done(((bf16[80,1920]{1,0:T(8,128)(2,1)}), bf16[1280,1920]{1,0:T(8,128)(2,1)}) %all-gather.3.cloned.1.call-update) | async-done | bytes 4915216 | tf_op jit(solution)/shard_map/all_gather | solution.py:108
  66.4 4.1 %fusion.4 = bf16[1,256,1920]{2,1,0:T(8,128)(2,1)S(1)} fusion(bf16[1280,1920]{1,0:T(8,128)(2,1)} %all-gather.3.cloned.1.call-done, f32[1920]{0:T(1024)S(1)} %copy-done.2, bf16[256,1280]{1,0:T(8,128)(2,1)S(1)} %copy-done, bf16[256,1280]{1,0:T(8,128)(2,1)S(1)} %bitcast.37, f32[1280]{0:T(1024)S(1)} %copy-done.3, f32[1280]{0:T(1024)S(1)} %copy-done.4, ...), kind=kOutput, calls=%fused_computation.6 | convolution fusion | flops 1261895680 | bytes 7228928 | tf_op jit(solution)/shard_map/dot_general | solution.py:106
  71.2 2.2 %fusion.27 = (f32[8,256]{1,0:T(8,128)S(1)}, f32[8,256,256]{1,2,0:T(8,128)}) fusion(bf16[256,8,80]{0,2,1:T(8,128)(2,1)S(1)} %bitcast.42, bf16[256,8,80]{0,2,1:T(8,128)(2,1)S(1)} %bitcast.43), kind=kOutput, calls=%fused_computation.55 | convolution fusion | flops 85459200 | bytes 2760704 | tf_op jit(solution)/shard_map/vmap()/sub | solution.py:56
  73.3 2.0 %convolution_convert_fusion = bf16[8,80,256]{2,1,0:T(8,128)(2,1)S(1)} fusion(bf16[256,8,80]{0,2,1:T(8,128)(2,1)S(1)} %bitcast.44, f32[8,256,256]{1,2,0:T(8,128)} %get-tuple-element.111, f32[8,256]{1,0:T(8,128)S(1)} %get-tuple-element.110), kind=kOutput, calls=%fused_computation.14 | convolution fusion | flops 85098496 | bytes 2760704 | tf_op jit(solution)/shard_map/vmap(hqk,khd->qhd)/dot_general | solution.py:58
  75.3 31.7 %all-gather.5.cloned.1.call-done = bf16[1280,640]{1,0:T(8,128)(2,1)} async-done(((bf16[80,640]{1,0:T(8,128)(2,1)}), bf16[1280,640]{1,0:T(8,128)(2,1)}) %all-gather.5.cloned.1.call-update) | async-done | bytes 1638416 | tf_op jit(solution)/shard_map/all_gather | solution.py:117
  107.0 2.3 %fusion.28 = (bf16[256,1280]{1,0:T(8,128)(2,1)S(1)}, f32[256,1280]{1,0:T(8,128)S(1)}) fusion(f32[1280]{0:T(1024)S(1)} %copy-done.1, bf16[256,640]{0,1:T(8,128)(2,1)S(1)} %bitcast.41, bf16[1280,640]{1,0:T(8,128)(2,1)} %all-gather.5.cloned.1.call-done, bf16[256,1280]{1,0:T(8,128)(2,1)S(1)} %copy-done, bf16[256,1280]{1,0:T(8,128)(2,1)S(1)} %bitcast.38, ...), kind=kOutput, calls=%fused_computation.56 | convolution fusion | flops 421724160 | bytes 5249024 | tf_op jit(solution)/shard_map/dot_general | solution.py:115
  109.3 2.4 %collective-permute-start.4 = (bf16[4,16,1280]{2,1,0:T(8,128)(2,1)S(1)}, bf16[4,16,1280]{2,1,0:T(8,128)(2,1)S(1)}, u32[]{:S(2)}, u32[]{:S(2)}) collective-permute-start(bf16[4,16,1280]{2,1,0:T(8,128)(2,1)S(1)} %bitcast.46), channel_id=1, source_target_pairs={{0,2},{2,4},{4,6},{6,8},{8,10},{10,12},{12,14},{1,3},{3,5},{5,7},{... | collective-permute-start | bytes 491528 | tf_op jit(solution)/shard_map/ppermute | solution.py:17
  111.8 1.8 %collective-permute-start.10 = (bf16[8,4]{1,0:T(8,128)(2,1)S(1)}, bf16[8,4]{1,0:T(8,128)(2,1)S(1)}, u32[]{:S(2)}, u32[]{:S(2)}) collective-permute-start(bf16[8,4]{1,0:T(8,128)(2,1)S(1)} %get-tuple-element.108), channel_id=1, source_target_pairs={{0,1},{2,3},{4,5},{6,7},{8,9},{10,11},{12,13},{14,15},{16,17},{18,... | collective-permute-start | bytes 200 | tf_op jit(solution)/shard_map/ppermute | solution.py:17
  113.6 1.3 collective-permute-start.11
  115.0 1.3 collective-permute-start.5
  116.4 7.5 %collective-permute-done.5 = bf16[4,16,1280]{2,1,0:T(8,128)(2,1)S(1)} collective-permute-done((bf16[4,16,1280]{2,1,0:T(8,128)(2,1)S(1)}, bf16[4,16,1280]{2,1,0:T(8,128)(2,1)S(1)}, u32[]{:S(2)}, u32[]{:S(2)}) %collective-permute-start.5) | collective-permute-done | bytes 163872 | tf_op jit(solution)/shard_map/ppermute | solution.py:17
  124.0 2.0 %collective-permute-start.6 = (bf16[8,4,1280]{2,1,0:T(4,128)(2,1)S(1)}, bf16[8,4,1280]{2,1,0:T(4,128)(2,1)S(1)}, u32[]{:S(2)}, u32[]{:S(2)}) collective-permute-start(bf16[8,4,1280]{2,1,0:T(4,128)(2,1)S(1)} %get-tuple-element.100), channel_id=1, source_target_pairs={{0,1},{2,3},{4,5},{6,7},{8,9},{10,11},{12,13},{14,15},{16,17},{18,... | collective-permute-start | bytes 245768 | tf_op jit(solution)/shard_map/ppermute | solution.py:17
  126.1 1.3 collective-permute-start.7
  127.5 1.8 %collective-permute-done.7 = bf16[8,4,1280]{2,1,0:T(4,128)(2,1)S(1)} collective-permute-done((bf16[8,4,1280]{2,1,0:T(4,128)(2,1)S(1)}, bf16[8,4,1280]{2,1,0:T(4,128)(2,1)S(1)}, u32[]{:S(2)}, u32[]{:S(2)}) %collective-permute-start.7) | collective-permute-done | bytes 81952 | tf_op jit(solution)/shard_map/ppermute | solution.py:17
  129.2 0.8 fusion.13
  (57 shorter events, 4.8 us)
Async XLA Ops:
  6.5 59.8 %all-gather.3.cloned.1.call-start = ((), (), s32[]{:S(2)}) async-start(), calls=%async_computation | async-start | bytes 5222400 | tf_op jit(solution)/shard_map/all_gather | solution.py:108
  7.3 99.8 %all-gather.5.cloned.1.call-start = ((), (), s32[]{:S(2)}) async-start(), calls=%async_computation.1 | async-start | bytes 1740800 | tf_op jit(solution)/shard_map/all_gather | solution.py:117
  8.2 13.8 %collective-permute-start = (bf16[4,8,1280]{2,1,0:T(8,128)(2,1)S(1)}, bf16[4,8,1280]{2,1,0:T(8,128)(2,1)S(1)}, u32[]{:S(2)}, u32[]{:S(2)}) collective-permute-start(bf16[4,8,1280]{2,1,0:T(8,128)(2,1)S(1)} %get-tuple-element.105), channel_id=1, source_target_pairs={{0,2},{2,4},{4,6},{6,8},{8,10},{10,12},{12,14},{1,3},{3,5},{5,7},{... | collective-permute-start | bytes 245768 | tf_op jit(solution)/shard_map/ppermute | solution.py:25
  13.1 10.0 %collective-permute-start.1 = (bf16[4,8,1280]{2,1,0:T(8,128)(2,1)S(1)}, bf16[4,8,1280]{2,1,0:T(8,128)(2,1)S(1)}, u32[]{:S(2)}, u32[]{:S(2)}) collective-permute-start(bf16[4,8,1280]{2,1,0:T(8,128)(2,1)S(1)} %get-tuple-element.104), channel_id=1, source_target_pairs={{2,0},{4,2},{6,4},{8,6},{10,8},{12,10},{14,12},{3,1},{5,3},{7,5},{... | collective-permute-start | bytes 245768 | tf_op jit(solution)/shard_map/ppermute | solution.py:28
  15.3 6.7 %collective-permute-start.8 = (bf16[4,16]{1,0:T(4,128)(2,1)S(1)}, bf16[4,16]{1,0:T(4,128)(2,1)S(1)}, u32[]{:S(2)}, u32[]{:S(2)}) collective-permute-start(bf16[4,16]{1,0:T(4,128)(2,1)S(1)} %get-tuple-element.107), channel_id=1, source_target_pairs={{0,2},{2,4},{4,6},{6,8},{8,10},{10,12},{12,14},{1,3},{3,5},{5,7},{... | collective-permute-start | bytes 392 | tf_op jit(solution)/shard_map/ppermute | solution.py:17
  19.9 6.0 %collective-permute-start.9 = (bf16[4,16]{1,0:T(4,128)(2,1)S(1)}, bf16[4,16]{1,0:T(4,128)(2,1)S(1)}, u32[]{:S(2)}, u32[]{:S(2)}) collective-permute-start(bf16[4,16]{1,0:T(4,128)(2,1)S(1)} %get-tuple-element.106), channel_id=1, source_target_pairs={{2,0},{4,2},{6,4},{8,6},{10,8},{12,10},{14,12},{3,1},{5,3},{7,5},{... | collective-permute-start | bytes 392 | tf_op jit(solution)/shard_map/ppermute | solution.py:17
  22.1 6.1 %copy-start = (bf16[256,1280]{1,0:T(8,128)(2,1)S(1)}, bf16[256,1280]{1,0:T(8,128)(2,1)}, u32[]{:S(2)}) copy-start(bf16[256,1280]{1,0:T(8,128)(2,1)} %param.26) | copy-start | bytes 1966084
  23.2 2.7 %collective-permute-start.2 = (bf16[16,4,1280]{2,1,0:T(4,128)(2,1)S(1)}, bf16[16,4,1280]{2,1,0:T(4,128)(2,1)S(1)}, u32[]{:S(2)}, u32[]{:S(2)}) collective-permute-start(bf16[16,4,1280]{2,1,0:T(4,128)(2,1)S(1)} %get-tuple-element.102), channel_id=1, source_target_pairs={{0,1},{2,3},{4,5},{6,7},{8,9},{10,11},{12,13},{14,15},{16,17},{18,... | collective-permute-start | bytes 491528 | tf_op jit(solution)/shard_map/ppermute | solution.py:25
  24.6 3.3 %collective-permute-start.3 = (bf16[16,4,1280]{2,1,0:T(4,128)(2,1)S(1)}, bf16[16,4,1280]{2,1,0:T(4,128)(2,1)S(1)}, u32[]{:S(2)}, u32[]{:S(2)}) collective-permute-start(bf16[16,4,1280]{2,1,0:T(4,128)(2,1)S(1)} %get-tuple-element.103), channel_id=1, source_target_pairs={{1,0},{3,2},{5,4},{7,6},{9,8},{11,10},{13,12},{15,14},{17,16},{19,... | collective-permute-start | bytes 491528 | tf_op jit(solution)/shard_map/ppermute | solution.py:28
  28.2 38.2 %copy-start.2 = (f32[1920]{0:T(1024)S(1)}, f32[1920]{0:T(1024)}, u32[]{:S(2)}) copy-start(f32[1920]{0:T(1024)} %param.30) | copy-start | bytes 23044
  28.2 38.2 %copy-start.3 = (f32[1280]{0:T(1024)S(1)}, f32[1280]{0:T(1024)}, u32[]{:S(2)}) copy-start(f32[1280]{0:T(1024)} %param.28) | copy-start | bytes 15364
  28.2 38.2 %copy-start.4 = (f32[1280]{0:T(1024)S(1)}, f32[1280]{0:T(1024)}, u32[]{:S(2)}) copy-start(f32[1280]{0:T(1024)} %param.27) | copy-start | bytes 15364
  73.3 33.7 %copy-start.1 = (f32[1280]{0:T(1024)S(1)}, f32[1280]{0:T(1024)}, u32[]{:S(2)}) copy-start(f32[1280]{0:T(1024)} %param.32) | copy-start | bytes 15364
  109.3 7.0 %collective-permute-start.4 = (bf16[4,16,1280]{2,1,0:T(8,128)(2,1)S(1)}, bf16[4,16,1280]{2,1,0:T(8,128)(2,1)S(1)}, u32[]{:S(2)}, u32[]{:S(2)}) collective-permute-start(bf16[4,16,1280]{2,1,0:T(8,128)(2,1)S(1)} %bitcast.46), channel_id=1, source_target_pairs={{0,2},{2,4},{4,6},{6,8},{8,10},{10,12},{12,14},{1,3},{3,5},{5,7},{... | collective-permute-start | bytes 491528 | tf_op jit(solution)/shard_map/ppermute | solution.py:17
  111.8 15.6 %collective-permute-start.10 = (bf16[8,4]{1,0:T(8,128)(2,1)S(1)}, bf16[8,4]{1,0:T(8,128)(2,1)S(1)}, u32[]{:S(2)}, u32[]{:S(2)}) collective-permute-start(bf16[8,4]{1,0:T(8,128)(2,1)S(1)} %get-tuple-element.108), channel_id=1, source_target_pairs={{0,1},{2,3},{4,5},{6,7},{8,9},{10,11},{12,13},{14,15},{16,17},{18,... | collective-permute-start | bytes 200 | tf_op jit(solution)/shard_map/ppermute | solution.py:17
  113.6 13.7 %collective-permute-start.11 = (bf16[8,4]{1,0:T(8,128)(2,1)S(1)}, bf16[8,4]{1,0:T(8,128)(2,1)S(1)}, u32[]{:S(2)}, u32[]{:S(2)}) collective-permute-start(bf16[8,4]{1,0:T(8,128)(2,1)S(1)} %get-tuple-element.109), channel_id=1, source_target_pairs={{1,0},{3,2},{5,4},{7,6},{9,8},{11,10},{13,12},{15,14},{17,16},{19,... | collective-permute-start | bytes 200 | tf_op jit(solution)/shard_map/ppermute | solution.py:17
  115.0 8.8 %collective-permute-start.5 = (bf16[4,16,1280]{2,1,0:T(8,128)(2,1)S(1)}, bf16[4,16,1280]{2,1,0:T(8,128)(2,1)S(1)}, u32[]{:S(2)}, u32[]{:S(2)}) collective-permute-start(bf16[4,16,1280]{2,1,0:T(8,128)(2,1)S(1)} %bitcast.45), channel_id=1, source_target_pairs={{2,0},{4,2},{6,4},{8,6},{10,8},{12,10},{14,12},{3,1},{5,3},{7,5},{... | collective-permute-start | bytes 491528 | tf_op jit(solution)/shard_map/ppermute | solution.py:17
  124.0 3.4 %collective-permute-start.6 = (bf16[8,4,1280]{2,1,0:T(4,128)(2,1)S(1)}, bf16[8,4,1280]{2,1,0:T(4,128)(2,1)S(1)}, u32[]{:S(2)}, u32[]{:S(2)}) collective-permute-start(bf16[8,4,1280]{2,1,0:T(4,128)(2,1)S(1)} %get-tuple-element.100), channel_id=1, source_target_pairs={{0,1},{2,3},{4,5},{6,7},{8,9},{10,11},{12,13},{14,15},{16,17},{18,... | collective-permute-start | bytes 245768 | tf_op jit(solution)/shard_map/ppermute | solution.py:17
  126.1 3.2 %collective-permute-start.7 = (bf16[8,4,1280]{2,1,0:T(4,128)(2,1)S(1)}, bf16[8,4,1280]{2,1,0:T(4,128)(2,1)S(1)}, u32[]{:S(2)}, u32[]{:S(2)}) collective-permute-start(bf16[8,4,1280]{2,1,0:T(4,128)(2,1)S(1)} %get-tuple-element.101), channel_id=1, source_target_pairs={{1,0},{3,2},{5,4},{7,6},{9,8},{11,10},{13,12},{15,14},{17,16},{19,... | collective-permute-start | bytes 245768 | tf_op jit(solution)/shard_map/ppermute | solution.py:17
Sparse Core Ops, SparseCore 0:
  9.5 56.8 all-gather.2
  68.5 38.4 all-gather.4
where the time goes:
time: 137 us
  waiting for transfers between devices  81.1 us (59%)
  starting transfers between devices  24.7 us (18%)
  between operations  13.7 us (10%)
  matrix products  10.6 us (8%)
  other arithmetic  3.6 us (3%)
  local copies, waits for them, and re-layouts  3.12 us (2%)
    all_gather x1, waiting for transfers between devices, body(): lax.all_gather(w_qkv, ('row', 'col'), axis=0, tiled=True)  37.5 us
    all_gather x1, waiting for transfers between devices, body(): lax.all_gather(w_out, ('row', 'col'), axis=0, tiled=True)  31.7 us
    ppermute x8, starting transfers between devices, shifted(): lax.ppermute(value, axis, [(source, source + steps) for source in range(i...  15.9 us
    ppermute x8, waiting for transfers between devices, shifted(): lax.ppermute(value, axis, [(source, source + steps) for source in range(i...  9.3 us
    ppermute x2, starting transfers between devices, extended(): lax.ppermute(lax.slice_in_dim(block, block.shape[dim] - width, None, axis...  6.17 us
    dot_general x1, matrix products, body(): jnp.dot(normed, lax.all_gather(w_qkv, ('row', 'col'), axis=0, tiled=True)...  4.14 us
  transfers between devices with their start and end apart: 14, of which 6 were waited for; matrix products, arithmetic and copies ran while one was open for 10% of the time, Pallas kernels for 0%

commit v1 on v0

--- a/solution.py
+++ b/solution.py
@@ -1,14 +1,444 @@
+import functools
+
 import jax
 import jax.numpy as jnp
 from jax import lax
+from jax.experimental import pallas as pl
+from jax.experimental.pallas import tpu as pltpu
 from jax.sharding import PartitionSpec as P
 
 HEADS = 8
-
-
 EPSILON = 1e-06
 SPREAD = 4.0
 FLOOR = 0.25
+LANES = 128
+MESH = pl.DeviceIdType.MESH
+
+
+def kernel(
+    rows,
+    emb_ref, pos_ref, gain_ref, bias_ref, wq_ref, bq_ref, wo_ref, bo_ref, valid_ref,
+    out_ref,
+    eb, vb, wq_all, wo_all, nrm, proj, posr, base, wcol, att, rim_out, rim_in,
+    top_out, top_in, bot_out, bot_in, send_sems, recv_sems, local_sems,
+):
+    g, r, c = lax.axis_index("groups"), lax.axis_index("row"), lax.axis_index("col")
+    half = rows // 2
+    tile, _, width = emb_ref.shape
+    rim = tile // 2
+    win = 2 * tile
+    tok = win * win
+    shard = wq_ref.shape[0]
+    qkv = wq_ref.shape[1]
+    hd = wo_ref.shape[1]
+    head = hd // HEADS
+    p = jnp.where(r % 2 == 0, r // 2, rows - 1 - r // 2)
+
+    def row_at(position):
+        q = lax.rem(position + 2 * rows, rows)
+        return jnp.where(q < half, 2 * q, 2 * (rows - 1 - q) + 1)
+
+    d = 1 - 2 * c
+    ahead, behind = row_at(p + d), row_at(p - d)
+    above, below = lax.rem(r + rows - 1, rows), lax.rem(r + 1, rows)
+    other = 1 - c
+    to_core, to_y = (g, r, other), (1 - g, r, c)
+
+    names = {}
+
+    def copy(name, src, dst, device):
+        at = names.setdefault(name, len(names))
+        return pltpu.make_async_remote_copy(
+            src_ref=src, dst_ref=dst, send_sem=send_sems.at[at], recv_sem=recv_sems.at[at],
+            device_id=device, device_id_type=MESH,
+        )
+
+    pending = []
+
+    def start(name, src, dst, device):
+        item = copy(name, src, dst, device)
+        item.start()
+        pending.append(item)
+
+    def arrived(name, dst):
+        copy(name, dst, dst, to_core).wait_recv()
+
+    barrier = pltpu.get_barrier_semaphore()
+    peers = [to_core, to_y, (g, ahead, c), (g, behind, c),
+             (g, above, c), (g, below, c), (g, above, other), (g, below, other)]
+    for peer in peers:
+        pl.semaphore_signal(barrier, inc=1, device_id=peer, device_id_type=MESH)
+    pl.semaphore_wait(barrier, len(peers))
+
+    own_rows = pl.ds(rim, tile)
+    halo_down = copy("hd", emb_ref.at[pl.ds(tile - rim, rim)], eb.at[0, pl.ds(0, rim)], (g, below, c))
+    halo_up = copy("hu", emb_ref.at[pl.ds(0, rim)], eb.at[0, pl.ds(rim + tile, rim)], (g, above, c))
+
+    @pl.when(r < rows - 1)
+    def _():
+        halo_down.start()
+
+    @pl.when(r > 0)
+    def _():
+        halo_up.start()
+
+    start("ec", emb_ref, eb.at[1, own_rows], to_core)
+    start("v0", valid_ref, vb.at[0], (g, below, c))
+    start("v2", valid_ref, vb.at[2], (g, above, c))
+    start("v3", valid_ref, vb.at[3], (g, below, other))
+    start("v4", valid_ref, vb.at[4], to_core)
+    start("v5", valid_ref, vb.at[5], (g, above, other))
+
+    class Stream:
+        def __init__(self, name, ref, gathered):
+            self.name, self.ref, self.all = name, ref, gathered
+            units = ref.shape[1] // LANES
+            side = (units + 1) // 3
+            self.ring_w, self.y_w = (units - side) * LANES, side * LANES
+            self.ring = pl.ds(pl.multiple_of(g * self.y_w, LANES), self.ring_w)
+            self.y_out = pl.ds(pl.multiple_of(g * self.ring_w, LANES), self.y_w)
+            self.y_in = pl.ds(pl.multiple_of((1 - g) * self.ring_w, LANES), self.y_w)
+
+        def shard_row(self, way, step):
+            return row_at(p - d * (step + 1)) if way == 0 else row_at(p + d * (step + 1))
+
+        def place(self, row, core, cols):
+            return self.all.at[row, core, :, cols]
+
+        def send(self, way, step):
+            row = r if step == 0 else self.shard_row(way, step - 1)
+            src = self.ref.at[:, self.ring] if step == 0 else self.place(row, c, self.ring)
+            device = (g, ahead if way == 0 else behind, c)
+            start(f"{self.name}r{way}{step}", src, self.place(row, c, self.ring), device)
+
+        def begin(self):
+            self.send(0, 0)
+            self.send(1, 0)
+
+        def own(self):
+            start(f"{self.name}o", self.ref, self.all.at[r, c], to_core)
+
+        def ways(self, step):
+            return (0, 1) if step < half - 1 else (0,)
+
+        def ring_recv(self, step):
+            for way in self.ways(step):
+                row = self.shard_row(way, step)
+                here = self.place(row, c, self.ring)
+                arrived(f"{self.name}r{way}{step}", here)
+                if way in self.ways(step + 1) and step + 1 < half:
+                    self.send(way, step + 1)
+                if step < half - 1:
+                    side = self.place(row, c, self.y_out)
+                    start(f"{self.name}y{way}{step}", side, side, to_y)
+                start(f"{self.name}c{way}{step}", here, here, to_core)
+
+        def y_recv(self, step):
+            for way in self.ways(step):
+                row = self.shard_row(way, step)
+                here = self.place(row, c, self.y_in)
+                if step < half - 1:
+                    arrived(f"{self.name}y{way}{step}", here)
+                    if step == half - 2 and way == 0:
+                        start(f"{self.name}l", here, here, (g, ahead, c))
+                else:
+                    arrived(f"{self.name}l", here)
+                start(f"{self.name}d{way}{step}", here, here, to_core)
+
+        def core_recv(self, step):
+            for way in self.ways(step):
+                row = row_at(p + d * (step + 1)) if way == 0 else row_at(p - d * (step + 1))
+                arrived(f"{self.name}c{way}{step}", self.place(row, other, self.ring))
+                arrived(f"{self.name}d{way}{step}", self.place(row, other, self.y_in))
+
+        def own_recv(self):
+            arrived(f"{self.name}o", self.all.at[r, other])
+
+    qs, ws = Stream("q", wq_ref, wq_all), Stream("w", wo_ref, wo_all)
+    qs.begin()
+    qs.own()
+    ws.own()
+    mine = [
+        pltpu.make_async_copy(wq_ref, wq_all.at[r, c], local_sems.at[0]),
+        pltpu.make_async_copy(wo_ref, wo_all.at[r, c], local_sems.at[1]),
+    ]
+    for item in mine:
+        item.start()
+
+    eb[0, rim:rim + tile] = emb_ref[...]
+
+    @pl.when(r == 0)
+    def _():
+        eb[0, 0:rim] = jnp.zeros((rim, tile, width), eb.dtype)
+        eb[1, 0:rim] = jnp.zeros((rim, tile, width), eb.dtype)
+
+    @pl.when(r == rows - 1)
+    def _():
+        eb[0, rim + tile:] = jnp.zeros((rim, tile, width), eb.dtype)
+        eb[1, rim + tile:] = jnp.zeros((rim, tile, width), eb.dtype)
+
+    arrived("ec", eb.at[1, own_rows])
+    fwd_top = copy("ft", eb.at[0, pl.ds(0, rim)], eb.at[1, pl.ds(0, rim)], to_core)
+    fwd_bot = copy("fb", eb.at[0, pl.ds(rim + tile, rim)], eb.at[1, pl.ds(rim + tile, rim)], to_core)
+
+    @pl.when(r > 0)
+    def _():
+        halo_down.wait_recv()
+        fwd_top.start()
+
+    @pl.when(r < rows - 1)
+    def _():
+        halo_up.wait_recv()
+        fwd_bot.start()
+
+    @pl.when(r > 0)
+    def _():
+        fwd_top.wait_recv()
+
+    @pl.when(r < rows - 1)
+    def _():
+        fwd_bot.wait_recv()
+
+    gain, bias = gain_ref[...], bias_ref[...]
+    span = 2 * shard
+    per = rim
+    place = lax.broadcasted_iota(jnp.int32, (per, tile, 1), 1)
+    rim_ok = jnp.where(c == 0, place, tile - 1 - place) < rim
+
+    def norm_block(block, carry):
+        at = pl.ds(block * per, per)
+        left = eb[0, at].astype(jnp.float32)
+        right = jnp.where(rim_ok, eb[1, at].astype(jnp.float32), 0.0)
+        pos = pos_ref[pl.ds(pl.multiple_of(block * per * win, per * win), per * win)]
+        pos = pos.astype(jnp.float32).reshape(per, win, width)
+        pos = pltpu.roll(pos, win - rim, 1)
+        posr[at] = pos
+        x = (jnp.concatenate([left, right], axis=1) + pos).reshape(per * win, width)
+        x = x - jnp.mean(x, axis=-1, keepdims=True)
+        variance = jnp.mean(x * x, axis=-1, keepdims=True)
+        x = x * lax.rsqrt(variance + EPSILON) * gain + bias
+        there = pl.ds(pl.multiple_of(block * per * win, per * win), per * win)
+        for k in range(rows):
+            nrm[k, there] = x[:, k * span:(k + 1) * span].astype(jnp.bfloat16)
+        return carry
+
+    lax.fori_loop(0, win // per, norm_block, 0)
+
+    for slot, name in ((0, "v0"), (2, "v2"), (3, "v3"), (4, "v4"), (5, "v5")):
+        arrived(name, vb.at[slot])
+    counts = [vb[0, 0], valid_ref[0], vb[2, 0], vb[3, 0], vb[4, 0], vb[5, 0]]
+    counts = jnp.concatenate(
+        [v.astype(jnp.float32) for v in counts] + [jnp.zeros((2, tok), jnp.float32)], axis=0
+    ).astype(jnp.bfloat16)
+    t_row = lax.broadcasted_iota(jnp.int32, (tok, tok), 0)
+    t_col = lax.broadcasted_iota(jnp.int32, (tok, tok), 1)
+    base_row = t_row // win * win
+    pick = (t_col == base_row + (t_row - base_row + rim) % win).astype(jnp.float32).astype(jnp.bfloat16)
+    counts = lax.dot_general(pick, counts, (((1,), (1,)), ((), ())), preferred_element_type=jnp.float32)
+    t = lax.broadcasted_iota(jnp.int32, (tok, 1), 0)
+    oi = (t // win).astype(jnp.float32) - (win - 1) / 2.0
+    oj = ((t % win + rim) % win).astype(jnp.float32) - (win - 1) / 2.0
+    gauss = jnp.exp(-(oi * oi + oj * oj) / (2.0 * SPREAD * SPREAD))
+    weights = gauss * counts / 196.0
+    wcol[...] = weights
+    grid = weights.reshape(win, win, 8)
+    near = grid[:, :tile].reshape(win * tile, 8)
+    far = grid[:, tile:].reshape(win * tile, 8)
+    u = lax.broadcasted_iota(jnp.int32, (win * tile, 1), 0) % tile
+    fold_ok = jnp.where(c == 1, u, tile - 1 - u) < rim
+    far = jnp.where(fold_ok, far, 0.0)
+    low, high = rim * tile, (rim + tile) * tile
+    has_above, has_below = r > 0, r < rows - 1
+    near0, far0 = near[low:high, 1:2], far[low:high, 4:5]
+    near_a = jnp.where(has_above, near[high:, 0:1], 0.0)
+    far_a = jnp.where(has_above, far[high:, 3:4], 0.0)
+    near_b = jnp.where(has_below, near[:low, 2:3], 0.0)
+    far_b = jnp.where(has_below, far[:low, 5:6], 0.0)
+    denom = near0 + far0 + jnp.concatenate([near_a + far_a, near_b + far_b], axis=0)
+
+    qs.ring_recv(0)
+    ws.begin()
+
+    def flat(lo, hi, a, b):
+        return posr[lo:hi, a:b].reshape((hi - lo) * (b - a), width)
+
+    total = denom * (emb_ref[...].astype(jnp.float32).reshape(tile * tile, width) + bo_ref[...])
+    total += near0 * flat(rim, rim + tile, 0, tile) + far0 * flat(rim, rim + tile, tile, win)
+    base[...] = total
+    base[0:low] += near_a * flat(rim + tile, win, 0, tile) + far_a * flat(rim + tile, win, tile, win)
+    base[low:] += near_b * flat(0, rim, 0, tile) + far_b * flat(0, rim, tile, win)
+
+    block_n = qkv // 3
+
+    def multiply(row, first=False):
+        def part(n, carry):
+            cols = pl.ds(pl.multiple_of(n * block_n, LANES), block_n)
+            got = jnp.dot(
+                nrm[row], wq_all[row, :, :, cols].reshape(span, block_n),
+                preferred_element_type=jnp.float32,
+            )
+            if first:
+                proj[:, cols] = got + bq_ref[:, cols]
+            else:
+                proj[:, cols] += got
+            return carry
+
+        lax.fori_loop(0, 3, part, 0)
+
+    for item in mine:
+        item.wait()
+    qs.own_recv()
+    multiply(r, True)
+
+    for step in range(1, half):
+        last = step == half - 1
+        if not last:
+            qs.ring_recv(step)
+        qs.y_recv(step - 1)
+        qs.core_recv(step - 1)
+        multiply(row_at(p - step))
+        multiply(row_at(p + step))
+        if last:
+            qs.ring_recv(step)
+        ws.ring_recv(step - 1)
+        if step >= 2:
+            ws.y_recv(step - 2)
+    qs.y_recv(half - 1)
+    qs.core_recv(half - 1)
+    multiply(row_at(p + half))
+
+    def attend(h):
+        lo, hi = h * head, (h + 1) * head
+        a, b = lo // LANES * LANES, -(-hi // LANES) * LANES
+        lane = lax.broadcasted_iota(jnp.int32, (1, b - a), 1) + a
+        inside = (lane >= lo) & (lane < hi)
+        q = jnp.where(inside, proj[:, a:b], 0.0).astype(jnp.bfloat16)
+        k = proj[:, hd + a:hd + b].astype(jnp.bfloat16)
+        v = proj[:, 2 * hd + a:2 * hd + b].astype(jnp.bfloat16)
+        scores = lax.dot_general(
+            q, k, (((1,), (1,)), ((), ())), preferred_element_type=jnp.float32
+        ) * head ** (-0.5)
+        expon = jnp.exp(scores - jnp.max(scores, axis=-1, keepdims=True))
+        probs = (expon / jnp.sum(expon, axis=-1, keepdims=True)).astype(jnp.bfloat16)
+        mixed = jnp.dot(probs, v, preferred_element_type=jnp.float32)
+        att[:, a:b] = mixed if lo == a else jnp.where(inside, mixed, att[:, a:b])
+
+    for h in range(HEADS // 2):
+        attend(h)
+    ws.y_recv(half - 2)
+    for h in range(HEADS // 2, HEADS):
+        attend(h)
+    ws.ring_recv(half - 1)
+
+    merged = att[...].astype(jnp.bfloat16).astype(jnp.float32) * wcol[:, 1:2]
+    merged = merged.reshape(win, win, hd)
+    rim_out[...] = merged[:, tile:].reshape(win * tile, hd).astype(jnp.bfloat16)
+    start("rc", rim_out, rim_in, to_core)
+    own = merged[:, :tile].reshape(win * tile, hd)
+    ws.y_recv(half - 1)
+    arrived("rc", rim_in)
+    own = own + jnp.where(fold_ok, rim_in[...].astype(jnp.float32), 0.0)
+    top_out[...] = own[:low].astype(jnp.bfloat16)
+    bot_out[...] = own[high:].astype(jnp.bfloat16)
+    send_top = copy("rt", top_out, bot_in, (g, above, c))
+    send_bot = copy("rb", bot_out, top_in, (g, below, c))
+
+    @pl.when(r > 0)
+    def _():
+        send_top.start()
+
+    @pl.when(r < rows - 1)
+    def _():
+        send_bot.start()
+
+    @pl.when(r == 0)
+    def _():
+        top_in[...] = jnp.zeros_like(top_in)
+
+    @pl.when(r == rows - 1)
+    def _():
+        bot_in[...] = jnp.zeros_like(bot_in)
+
+    for step in range(half):
+        ws.core_recv(step)
+    ws.own_recv()
+
+    @pl.when(r > 0)
+    def _():
+        send_bot.wait_recv()
+
+    @pl.when(r < rows - 1)
+    def _():
+        send_top.wait_recv()
+
+    own = own[low:high] + jnp.concatenate(
+        [top_in[...].astype(jnp.float32), bot_in[...].astype(jnp.float32)], axis=0
+    )
+    result = base[...] + lax.dot_general(
+        own.astype(jnp.bfloat16), wo_all[...].reshape(width, hd),
+        (((1,), (1,)), ((), ())), preferred_element_type=jnp.float32,
+    )
+    result = result / jnp.maximum(denom, FLOOR)
+    out_ref[...] = result.reshape(tile, tile, width).astype(out_ref.dtype)
+
+    for item in pending:
+        item.wait_send()
+
+    @pl.when(r > 0)
+    def _():
+        halo_up.wait_send()
+        fwd_top.wait_send()
+        send_top.wait_send()
+
+    @pl.when(r < rows - 1)
+    def _():
+        halo_down.wait_send()
+        fwd_bot.wait_send()
+        send_bot.wait_send()
+
+
+def fused(rows, embeddings, pos_embed, ln_gain, ln_bias, w_qkv, b_qkv, w_out, b_out, valid):
+    tile, _, width = embeddings.shape
+    win, rim = 2 * tile, tile // 2
+    tok = win * win
+    shard, qkv = w_qkv.shape
+    hd = w_out.shape[1]
+    copies = 8 * 8 * rows
+    bf16, f32 = jnp.bfloat16, jnp.float32
+    vmem = pl.BlockSpec(memory_space=pltpu.VMEM)
+    return pl.pallas_call(
+        functools.partial(kernel, rows),
+        out_shape=jax.ShapeDtypeStruct(embeddings.shape, bf16),
+        in_specs=[vmem] * 9,
+        out_specs=vmem,
+        scratch_shapes=[
+            pltpu.VMEM((2, win, tile, width), bf16),
+            pltpu.VMEM((6, 1, 1, tok), jnp.int32),
+            pltpu.VMEM((rows, 2, shard, qkv), bf16),
+            pltpu.VMEM((rows, 2, shard, hd), bf16),
+            pltpu.VMEM((rows, tok, 2 * shard), bf16),
+            pltpu.VMEM((tok, qkv), f32),
+            pltpu.VMEM((win, win, width), f32),
+            pltpu.VMEM((tile * tile, width), f32),
+            pltpu.VMEM((tok, 8), f32),
+            pltpu.VMEM((tok, hd), f32),
+            pltpu.VMEM((win * tile, hd), bf16),
+            pltpu.VMEM((win * tile, hd), bf16),
+            pltpu.VMEM((rim * tile, hd), bf16),
+            pltpu.VMEM((rim * tile, hd), bf16),
+            pltpu.VMEM((rim * tile, hd), bf16),
+            pltpu.VMEM((rim * tile, hd), bf16),
+            pltpu.SemaphoreType.DMA((96,)),
+            pltpu.SemaphoreType.DMA((96,)),
+            pltpu.SemaphoreType.DMA((2,)),
+        ],
+        compiler_params=pltpu.CompilerParams(
+            collective_id=0, has_side_effects=True, vmem_limit_bytes=48 * 1024 * 1024
+        ),
+    )(
+        embeddings, pos_embed, ln_gain.reshape(1, -1), ln_bias.reshape(1, -1), w_qkv,
+        b_qkv.reshape(1, -1), w_out, b_out.reshape(1, -1), valid,
+    )
 
 
 def shifted(value, axis, steps):
@@ -146,8 +576,19 @@
         P(),
         P(("groups", "row"), "col", None),
     )
+    rows = mesh.shape["row"]
+
+    def run(*arrays):
+        embeddings, w_qkv = arrays[0], arrays[4]
+        tile = embeddings.shape[1]
+        whole_tiles = w_qkv.shape[0] % 16 == 0 and embeddings.shape[0] == tile == 8
+        pairs = mesh.shape["groups"] == 2 and mesh.shape["col"] == 2
+        if whole_tiles and pairs and rows == 8:
+            return fused(rows, *arrays)
+        return body(*arrays)
+
     return jax.shard_map(
-        body,
+        run,
         mesh=mesh,
         in_specs=placed,
         out_specs=P(("groups", "row"), "col", None),

time: 137 us -> 55 us (0.40)
  waiting for transfers between devices: 81.1 us -> 0 us
  Pallas kernels: 0 us -> 47.2 us
  starting transfers between devices: 24.7 us -> 0 us
  between operations: 13.7 us -> 0.03 us
  matrix products: 10.6 us -> 0 us
  local copies, waits for them, and re-layouts: 3.12 us -> 7.31 us
  other arithmetic: 3.6 us -> 0 us
    all_gather x2 -> x0, waiting for transfers between devices: 69.2 us -> none  [the longest x1 37.5 us: body(): lax.all_gather(w_qkv, ('row', 'col'), axis=0, tiled=True)]
    pallas_call x0 -> x1, Pallas kernels: none -> 47.2 us  [fused(): pl.pallas_call(functools.partial(kernel, rows), out_shape=jax.ShapeDtypeS...]
    ppermute x12 -> x0, starting transfers between devices: 24.7 us -> none  [the longest x8 15.9 us: shifted(): lax.ppermute(value, axis, [(source, source + steps) for source in range(i...]
    ppermute x12 -> x0, waiting for transfers between devices: 11.2 us -> none  [the longest x8 9.3 us: shifted(): lax.ppermute(value, axis, [(source, source + steps) for source in range(i...]
    dot_general x3 -> x0, matrix products: 8.38 us -> none  [the longest x1 4.14 us: body(): jnp.dot(normed, lax.all_gather(w_qkv, ('row', 'col'), axis=0, tiled=True)...]
    unnamed x12 -> x17, local copies, waits for them, and re-layouts: 1.03 us -> 6.58 us
    convert_element_type x3 -> x0, other arithmetic: 2.2 us -> none  [the longest x2 1.38 us: body(): valid.reshape(tile_rows, rows_count).astype(jnp.float32)]
    sub x1 -> x0, matrix products: 2.17 us -> none  [attend(): expon = jnp.exp(scores - highest)]
  transfers between devices with their start and end apart: 14 -> 0, of which waited for: 6 -> 0; matrix products, arithmetic and copies ran while one was open for 10% -> 0% of each run, Pallas kernels for 0% -> 0%
where the time goes in v1:
time: 55 us; the launch traced here: 54.6 us
  Pallas kernels  47.2 us (86%)
  local copies, waits for them, and re-layouts  7.31 us (13%)
    pallas_call x1, Pallas kernels, fused(): pl.pallas_call(functools.partial(kernel, rows), out_shape=jax.ShapeDtypeS...  47.2 us
    unnamed x17, local copies, waits for them, and re-layouts  6.58 us

profile of v1, /device:TPU:0, one launch (start us, length us, event | category | flops | bytes accessed | tf_op | source)
XLA Modules:
  0.0 54.6 jit_solution(16929857985223127321)
XLA Ops:
  0.0 0.0 copy-start.6
  0.0 0.7 %reshape.12.gain_ref = f32[1,1280]{1,0:T(1,128)S(1)} reshape(f32[1280]{0:T(1024)} %param.11) | data formatting | bytes 10240 | tf_op jit(solution)/shard_map/reshape | solution.py:439
  0.7 0.0 copy-done.6
  0.7 0.0 copy-start.7
  0.7 0.7 %copy-done.7 = f32[1280]{0:T(1024)S(1)} copy-done((f32[1280]{0:T(1024)S(1)}, f32[1280]{0:T(1024)}, u32[]{:S(2)}) %copy-start.7) | copy-done | bytes 5144
  1.4 0.0 copy-start.5
  1.4 0.7 %copy-done.5 = f32[1920]{0:T(1024)S(1)} copy-done((f32[1920]{0:T(1024)S(1)}, f32[1920]{0:T(1024)}, u32[]{:S(2)}) %copy-start.5) | copy-done | bytes 7704
  2.1 0.0 copy-start.4
  2.1 0.7 %copy-done.4 = s32[1,1,256]{2,1,0:T(1,128)S(1)} copy-done((s32[1,1,256]{2,1,0:T(1,128)S(1)}, s32[1,1,256]{2,1,0:T(1,128)}, u32[]{:S(2)}) %copy-start.4) | copy-done | bytes 1048
  2.8 0.0 copy-start
  2.8 1.1 %copy-done = bf16[256,1280]{1,0:T(8,128)(2,1)S(1)} copy-done((bf16[256,1280]{1,0:T(8,128)(2,1)S(1)}, bf16[256,1280]{1,0:T(8,128)(2,1)}, u32[]{:S(2)}) %copy-start) | copy-done | bytes 655384
  3.9 0.0 copy-start.1
  3.9 1.0 %copy-done.1 = bf16[80,1920]{1,0:T(8,128)(2,1)S(1)} copy-done((bf16[80,1920]{1,0:T(8,128)(2,1)S(1)}, bf16[80,1920]{1,0:T(8,128)(2,1)}, u32[]{:S(2)}) %copy-start.1) | copy-done | bytes 307224
  4.8 0.0 copy-start.2
  4.9 0.9 %copy-done.2 = bf16[8,8,1280]{2,1,0:T(8,128)(2,1)S(1)} copy-done((bf16[8,8,1280]{2,1,0:T(8,128)(2,1)S(1)}, bf16[8,8,1280]{2,1,0:T(8,128)(2,1)}, u32[]{:S(2)}) %copy-start.2) | copy-done | bytes 163864
  5.8 0.0 copy-start.3
  5.8 0.9 %copy-done.3 = bf16[80,640]{1,0:T(8,128)(2,1)S(1)} copy-done((bf16[80,640]{1,0:T(8,128)(2,1)S(1)}, bf16[80,640]{1,0:T(8,128)(2,1)}, u32[]{:S(2)}) %copy-start.3) | copy-done | bytes 102424
  6.7 47.2 %shard_map.91 = bf16[8,8,1280]{2,1,0:T(8,128)(2,1)S(1)} custom-call(bf16[8,8,1280]{2,1,0:T(8,128)(2,1)S(1)} %copy-done.2, bf16[256,1280]{1,0:T(8,128)(2,1)S(1)} %copy-done, f32[1,1280]{1,0:T(1,128)S(1)} %reshape.12.gain_ref, f32[1,1280]{1,0:T(1,128)S(1)} %reshape.13.bias_ref, bf16[80,1920]{1,0:T(8,128)(2,1)S(1)} %copy-done.1, f32[1,1920]{1,0:T(1,128)S(1)} %reshape.14.bq_ref, ...), custom_call_target="tpu_custom_call" | custom-call | tf_op jit(solution)/shard_map/pallas_call | solution.py:409
  53.9 0.7 %copy.11 = bf16[8,8,1280]{2,1,0:T(8,128)(2,1)} copy(bf16[8,8,1280]{2,1,0:T(8,128)(2,1)S(1)} %shard_map.91) | data formatting | bytes 327680
  (3 shorter events, 0.0 us)
Async XLA Ops:
  0.0 0.7 %copy-start.6 = (f32[1280]{0:T(1024)S(1)}, f32[1280]{0:T(1024)}, u32[]{:S(2)}) copy-start(f32[1280]{0:T(1024)} %param.12) | copy-start | bytes 15364
  0.7 0.7 %copy-start.7 = (f32[1280]{0:T(1024)S(1)}, f32[1280]{0:T(1024)}, u32[]{:S(2)}) copy-start(f32[1280]{0:T(1024)} %param.16) | copy-start | bytes 15364
  1.4 0.7 %copy-start.5 = (f32[1920]{0:T(1024)S(1)}, f32[1920]{0:T(1024)}, u32[]{:S(2)}) copy-start(f32[1920]{0:T(1024)} %param.14) | copy-start | bytes 23044
  2.1 0.7 %copy-start.4 = (s32[1,1,256]{2,1,0:T(1,128)S(1)}, s32[1,1,256]{2,1,0:T(1,128)}, u32[]{:S(2)}) copy-start(s32[1,1,256]{2,1,0:T(1,128)} %valid_ref.1) | copy-start | bytes 3076
  2.8 1.1 %copy-start = (bf16[256,1280]{1,0:T(8,128)(2,1)S(1)}, bf16[256,1280]{1,0:T(8,128)(2,1)}, u32[]{:S(2)}) copy-start(bf16[256,1280]{1,0:T(8,128)(2,1)} %pos_ref.1) | copy-start | bytes 1966084
  3.9 1.0 %copy-start.1 = (bf16[80,1920]{1,0:T(8,128)(2,1)S(1)}, bf16[80,1920]{1,0:T(8,128)(2,1)}, u32[]{:S(2)}) copy-start(bf16[80,1920]{1,0:T(8,128)(2,1)} %wq_ref.1) | copy-start | bytes 921604
  4.8 0.9 %copy-start.2 = (bf16[8,8,1280]{2,1,0:T(8,128)(2,1)S(1)}, bf16[8,8,1280]{2,1,0:T(8,128)(2,1)}, u32[]{:S(2)}) copy-start(bf16[8,8,1280]{2,1,0:T(8,128)(2,1)} %emb_ref.1) | copy-start | bytes 491524
  5.8 0.9 %copy-start.3 = (bf16[80,640]{1,0:T(8,128)(2,1)S(1)}, bf16[80,640]{1,0:T(8,128)(2,1)}, u32[]{:S(2)}) copy-start(bf16[80,640]{1,0:T(8,128)(2,1)} %wo_ref.1) | copy-start | bytes 307204

commit v2 on v1

--- a/solution.py
+++ b/solution.py
@@ -17,8 +17,8 @@
 
 def kernel(
     rows,
-    emb_ref, pos_ref, gain_ref, bias_ref, wq_ref, bq_ref, wo_ref, bo_ref, valid_ref,
-    out_ref,
+    emb_ref, pos_hbm, gain_hbm, bias_hbm, wq_ref, bq_hbm, wo_ref, bo_hbm, valid_ref,
+    out_ref, pos_ref, gain_ref, bias_ref, bq_ref, bo_ref,
     eb, vb, wq_all, wo_all, nrm, proj, posr, base, wcol, att, rim_out, rim_in,
     top_out, top_in, bot_out, bot_in, send_sems, recv_sems, local_sems,
 ):
@@ -63,6 +63,17 @@
     def arrived(name, dst):
         copy(name, dst, dst, to_core).wait_recv()
 
+    own_rows = pl.ds(tile // 2, tile)
+    locals_ = []
+    for src, dst in (
+        (emb_ref, eb.at[0, own_rows]), (valid_ref, vb.at[1]), (pos_hbm, pos_ref),
+        (gain_hbm, gain_ref), (bias_hbm, bias_ref), (bo_hbm, bo_ref), (bq_hbm, bq_ref),
+        (wq_ref, wq_all.at[r, c]), (wo_ref, wo_all.at[r, c]),
+    ):
+        item = pltpu.make_async_copy(src, dst, local_sems.at[len(locals_)])
+        item.start()
+        locals_.append(item)
+
     barrier = pltpu.get_barrier_semaphore()
     peers = [to_core, to_y, (g, ahead, c), (g, behind, c),
              (g, above, c), (g, below, c), (g, above, other), (g, below, other)]
@@ -70,7 +81,6 @@
         pl.semaphore_signal(barrier, inc=1, device_id=peer, device_id_type=MESH)
     pl.semaphore_wait(barrier, len(peers))
 
-    own_rows = pl.ds(rim, tile)
     halo_down = copy("hd", emb_ref.at[pl.ds(tile - rim, rim)], eb.at[0, pl.ds(0, rim)], (g, below, c))
     halo_up = copy("hu", emb_ref.at[pl.ds(0, rim)], eb.at[0, pl.ds(rim + tile, rim)], (g, above, c))
 
@@ -158,14 +168,6 @@
     qs.begin()
     qs.own()
     ws.own()
-    mine = [
-        pltpu.make_async_copy(wq_ref, wq_all.at[r, c], local_sems.at[0]),
-        pltpu.make_async_copy(wo_ref, wo_all.at[r, c], local_sems.at[1]),
-    ]
-    for item in mine:
-        item.start()
-
-    eb[0, rim:rim + tile] = emb_ref[...]
 
     @pl.when(r == 0)
     def _():
@@ -199,7 +201,9 @@
     def _():
         fwd_bot.wait_recv()
 
-    gain, bias = gain_ref[...], bias_ref[...]
+    for item in locals_[:6]:
+        item.wait()
+    gain, bias = gain_ref[...].reshape(1, width), bias_ref[...].reshape(1, width)
     span = 2 * shard
     per = rim
     place = lax.broadcasted_iota(jnp.int32, (per, tile, 1), 1)
@@ -226,7 +230,7 @@
 
     for slot, name in ((0, "v0"), (2, "v2"), (3, "v3"), (4, "v4"), (5, "v5")):
         arrived(name, vb.at[slot])
-    counts = [vb[0, 0], valid_ref[0], vb[2, 0], vb[3, 0], vb[4, 0], vb[5, 0]]
+    counts = [vb[0, 0], vb[1, 0], vb[2, 0], vb[3, 0], vb[4, 0], vb[5, 0]]
     counts = jnp.concatenate(
         [v.astype(jnp.float32) for v in counts] + [jnp.zeros((2, tok), jnp.float32)], axis=0
     ).astype(jnp.bfloat16)
@@ -262,7 +266,10 @@
     def flat(lo, hi, a, b):
         return posr[lo:hi, a:b].reshape((hi - lo) * (b - a), width)
 
-    total = denom * (emb_ref[...].astype(jnp.float32).reshape(tile * tile, width) + bo_ref[...])
+    total = denom * (
+        eb[0, rim:rim + tile].astype(jnp.float32).reshape(tile * tile, width)
+        + bo_ref[...].reshape(1, width)
+    )
     total += near0 * flat(rim, rim + tile, 0, tile) + far0 * flat(rim, rim + tile, tile, win)
     base[...] = total
     base[0:low] += near_a * flat(rim + tile, win, 0, tile) + far_a * flat(rim + tile, win, tile, win)
@@ -278,14 +285,14 @@
                 preferred_element_type=jnp.float32,
             )
             if first:
-                proj[:, cols] = got + bq_ref[:, cols]
+                proj[:, cols] = got + bq_ref[cols].reshape(1, block_n)
             else:
                 proj[:, cols] += got
             return carry
 
         lax.fori_loop(0, 3, part, 0)
 
-    for item in mine:
+    for item in locals_[6:]:
         item.wait()
     qs.own_recv()
     multiply(r, True)
@@ -409,9 +416,14 @@
     return pl.pallas_call(
         functools.partial(kernel, rows),
         out_shape=jax.ShapeDtypeStruct(embeddings.shape, bf16),
-        in_specs=[vmem] * 9,
+        in_specs=[pl.BlockSpec(memory_space=pltpu.HBM)] * 9,
         out_specs=vmem,
         scratch_shapes=[
+            pltpu.VMEM((tok, width), bf16),
+            pltpu.VMEM((width,), f32),
+            pltpu.VMEM((width,), f32),
+            pltpu.VMEM((qkv,), f32),
+            pltpu.VMEM((width,), f32),
             pltpu.VMEM((2, win, tile, width), bf16),
             pltpu.VMEM((6, 1, 1, tok), jnp.int32),
             pltpu.VMEM((rows, 2, shard, qkv), bf16),
@@ -430,14 +442,13 @@
             pltpu.VMEM((rim * tile, hd), bf16),
             pltpu.SemaphoreType.DMA((96,)),
             pltpu.SemaphoreType.DMA((96,)),
-            pltpu.SemaphoreType.DMA((2,)),
+            pltpu.SemaphoreType.DMA((9,)),
         ],
         compiler_params=pltpu.CompilerParams(
-            collective_id=0, has_side_effects=True, vmem_limit_bytes=48 * 1024 * 1024
+            collective_id=0, has_side_effects=True, vmem_limit_bytes=67043328
         ),
     )(
-        embeddings, pos_embed, ln_gain.reshape(1, -1), ln_bias.reshape(1, -1), w_qkv,
-        b_qkv.reshape(1, -1), w_out, b_out.reshape(1, -1), valid,
+        embeddings, pos_embed, ln_gain, ln_bias, w_qkv, b_qkv, w_out, b_out, valid
     )
 
 

time: 55 us -> 50 us (0.909)
  local copies, waits for them, and re-layouts: 7.31 us -> 1.59 us
  Pallas kernels: 47.2 us -> 48.2 us
    unnamed x17 -> x1, local copies, waits for them, and re-layouts: 6.58 us -> 1.59 us
    pallas_call x1, Pallas kernels: 47.2 us -> 48.2 us  [fused(): pl.pallas_call(functools.partial(kernel, rows), out_shape=jax.ShapeDtypeS...]
    reshape x4 -> x0, local copies, waits for them, and re-layouts: 0.73 us -> none  [the longest x1 0.71 us: fused(): ln_gain.reshape(1, -1)]
where the time goes in v2:
time: 50 us; the launch traced here: 49.8 us
  Pallas kernels  48.2 us (96%)
  local copies, waits for them, and re-layouts  1.59 us (3%)
    pallas_call x1, Pallas kernels, fused(): pl.pallas_call(functools.partial(kernel, rows), out_shape=jax.ShapeDtypeS...  48.2 us
    unnamed x1, local copies, waits for them, and re-layouts  1.59 us

profile of v2, /device:TPU:0, one launch (start us, length us, event | category | flops | bytes accessed | tf_op | source)
XLA Modules:
  0.0 49.8 jit_solution(15976292689904490698)
XLA Ops:
  0.0 48.2 %shard_map.91 = bf16[8,8,1280]{2,1,0:T(8,128)(2,1)} custom-call(bf16[8,8,1280]{2,1,0:T(8,128)(2,1)} %emb_ref.1, bf16[256,1280]{1,0:T(8,128)(2,1)} %pos_hbm.1, f32[1280]{0:T(1024)} %gain_hbm.1, f32[1280]{0:T(1024)} %bias_hbm.1, bf16[80,1920]{1,0:T(8,128)(2,1)} %wq_ref.1, f32[1920]{0:T(1024)} %bq_hbm.1, bf16[80,640]{1,0:T(8,128)(2,1)} %wo_ref.1, f32[1280]{0:T(1024)} %bo_hbm.1, ...), custom_call_target="tpu_custom_call" | custom-call | tf_op jit(solution)/shard_map/pallas_call | solution.py:416
  48.2 1.6 %copy.11 = bf16[8,8,1280]{2,1,0:T(8,128)(2,1)} copy(bf16[8,8,1280]{2,1,0:T(8,128)(2,1)} %shard_map.91) | data formatting | bytes 327680

commit v3 on v2

--- a/solution.py
+++ b/solution.py
@@ -19,8 +19,8 @@
     rows,
     emb_ref, pos_hbm, gain_hbm, bias_hbm, wq_ref, bq_hbm, wo_ref, bo_hbm, valid_ref,
     out_ref, pos_ref, gain_ref, bias_ref, bq_ref, bo_ref,
-    eb, vb, wq_all, wo_all, nrm, proj, posr, base, wcol, att, rim_out, rim_in,
-    top_out, top_in, bot_out, bot_in, send_sems, recv_sems, local_sems,
+    eb, vb, wq_all, wo_all, nrm, proj, posr, base, wcol, att, near_out, near_in,
+    far_out, far_in, send_sems, recv_sems, local_sems,
 ):
     g, r, c = lax.axis_index("groups"), lax.axis_index("row"), lax.axis_index("col")
     half = rows // 2
@@ -75,39 +75,52 @@
         locals_.append(item)
 
     barrier = pltpu.get_barrier_semaphore()
-    peers = [to_core, to_y, (g, ahead, c), (g, behind, c),
-             (g, above, c), (g, below, c), (g, above, other), (g, below, other)]
-    for peer in peers:
+    has_above, has_below = r > 0, r < rows - 1
+    for peer in (to_core, to_y, (g, ahead, c), (g, behind, c)):
         pl.semaphore_signal(barrier, inc=1, device_id=peer, device_id_type=MESH)
-    pl.semaphore_wait(barrier, len(peers))
+
+    @pl.when(has_above)
+    def _():
+        for core in (c, other):
+            pl.semaphore_signal(barrier, inc=1, device_id=(g, above, core), device_id_type=MESH)
+
+    @pl.when(has_below)
+    def _():
+        for core in (c, other):
+            pl.semaphore_signal(barrier, inc=1, device_id=(g, below, core), device_id_type=MESH)
+
+    pl.semaphore_wait(barrier, 8 - 2 * (r == 0).astype(jnp.int32) - 2 * (r == rows - 1).astype(jnp.int32))
 
     halo_down = copy("hd", emb_ref.at[pl.ds(tile - rim, rim)], eb.at[0, pl.ds(0, rim)], (g, below, c))
     halo_up = copy("hu", emb_ref.at[pl.ds(0, rim)], eb.at[0, pl.ds(rim + tile, rim)], (g, above, c))
 
-    @pl.when(r < rows - 1)
+    count_down = [copy("v0", valid_ref, vb.at[0], (g, below, c)), copy("v3", valid_ref, vb.at[3], (g, below, other))]
+    count_up = [copy("v2", valid_ref, vb.at[2], (g, above, c)), copy("v5", valid_ref, vb.at[5], (g, above, other))]
+
+    @pl.when(has_below)
     def _():
         halo_down.start()
-
-    @pl.when(r > 0)
+        for item in count_down:
+            item.start()
+
+    @pl.when(has_above)
     def _():
         halo_up.start()
+        for item in count_up:
+            item.start()
 
     start("ec", emb_ref, eb.at[1, own_rows], to_core)
-    start("v0", valid_ref, vb.at[0], (g, below, c))
-    start("v2", valid_ref, vb.at[2], (g, above, c))
-    start("v3", valid_ref, vb.at[3], (g, below, other))
     start("v4", valid_ref, vb.at[4], to_core)
-    start("v5", valid_ref, vb.at[5], (g, above, other))
 
     class Stream:
-        def __init__(self, name, ref, gathered):
+        def __init__(self, name, ref, gathered, first, units):
             self.name, self.ref, self.all = name, ref, gathered
-            units = ref.shape[1] // LANES
             side = (units + 1) // 3
+            self.cols = pl.ds(first * LANES, units * LANES)
             self.ring_w, self.y_w = (units - side) * LANES, side * LANES
-            self.ring = pl.ds(pl.multiple_of(g * self.y_w, LANES), self.ring_w)
-            self.y_out = pl.ds(pl.multiple_of(g * self.ring_w, LANES), self.y_w)
-            self.y_in = pl.ds(pl.multiple_of((1 - g) * self.ring_w, LANES), self.y_w)
+            self.ring = pl.ds(pl.multiple_of(first * LANES + g * self.y_w, LANES), self.ring_w)
+            self.y_out = pl.ds(pl.multiple_of(first * LANES + g * self.ring_w, LANES), self.y_w)
+            self.y_in = pl.ds(pl.multiple_of(first * LANES + (1 - g) * self.ring_w, LANES), self.y_w)
 
         def shard_row(self, way, step):
             return row_at(p - d * (step + 1)) if way == 0 else row_at(p + d * (step + 1))
@@ -126,7 +139,7 @@
             self.send(1, 0)
 
         def own(self):
-            start(f"{self.name}o", self.ref, self.all.at[r, c], to_core)
+            start(f"{self.name}o", self.ref.at[:, self.cols], self.place(r, c, self.cols), to_core)
 
         def ways(self, step):
             return (0, 1) if step < half - 1 else (0,)
@@ -162,22 +175,31 @@
                 arrived(f"{self.name}d{way}{step}", self.place(row, other, self.y_in))
 
         def own_recv(self):
-            arrived(f"{self.name}o", self.all.at[r, other])
-
-    qs, ws = Stream("q", wq_ref, wq_all), Stream("w", wo_ref, wo_all)
-    qs.begin()
-    qs.own()
+            arrived(f"{self.name}o", self.place(r, other, self.cols))
+
+    units = qkv // LANES
+    early = (units + 1) // 2
+    parts = [Stream("q", wq_ref, wq_all, 0, early), Stream("k", wq_ref, wq_all, early, units - early)]
+    ws = Stream("w", wo_ref, wo_all, 0, hd // LANES)
+    for part in parts:
+        part.begin()
+    for part in parts:
+        part.own()
     ws.own()
 
     @pl.when(r == 0)
     def _():
         eb[0, 0:rim] = jnp.zeros((rim, tile, width), eb.dtype)
         eb[1, 0:rim] = jnp.zeros((rim, tile, width), eb.dtype)
+        vb[0] = jnp.zeros((1, 1, tok), vb.dtype)
+        vb[3] = jnp.zeros((1, 1, tok), vb.dtype)
 
     @pl.when(r == rows - 1)
     def _():
         eb[0, rim + tile:] = jnp.zeros((rim, tile, width), eb.dtype)
         eb[1, rim + tile:] = jnp.zeros((rim, tile, width), eb.dtype)
+        vb[2] = jnp.zeros((1, 1, tok), vb.dtype)
+        vb[5] = jnp.zeros((1, 1, tok), vb.dtype)
 
     arrived("ec", eb.at[1, own_rows])
     fwd_top = copy("ft", eb.at[0, pl.ds(0, rim)], eb.at[1, pl.ds(0, rim)], to_core)
@@ -200,6 +222,8 @@
     @pl.when(r < rows - 1)
     def _():
         fwd_bot.wait_recv()
+
+    parts[0].ring_recv(0)
 
     for item in locals_[:6]:
         item.wait()
@@ -228,8 +252,21 @@
 
     lax.fori_loop(0, win // per, norm_block, 0)
 
-    for slot, name in ((0, "v0"), (2, "v2"), (3, "v3"), (4, "v4"), (5, "v5")):
-        arrived(name, vb.at[slot])
+    parts[1].ring_recv(0)
+    ws.begin()
+
+    arrived("v4", vb.at[4])
+
+    @pl.when(has_above)
+    def _():
+        for item in count_down:
+            item.wait_recv()
+
+    @pl.when(has_below)
+    def _():
+        for item in count_up:
+            item.wait_recv()
+
     counts = [vb[0, 0], vb[1, 0], vb[2, 0], vb[3, 0], vb[4, 0], vb[5, 0]]
     counts = jnp.concatenate(
         [v.astype(jnp.float32) for v in counts] + [jnp.zeros((2, tok), jnp.float32)], axis=0
@@ -252,16 +289,12 @@
     fold_ok = jnp.where(c == 1, u, tile - 1 - u) < rim
     far = jnp.where(fold_ok, far, 0.0)
     low, high = rim * tile, (rim + tile) * tile
-    has_above, has_below = r > 0, r < rows - 1
     near0, far0 = near[low:high, 1:2], far[low:high, 4:5]
     near_a = jnp.where(has_above, near[high:, 0:1], 0.0)
     far_a = jnp.where(has_above, far[high:, 3:4], 0.0)
     near_b = jnp.where(has_below, near[:low, 2:3], 0.0)
     far_b = jnp.where(has_below, far[:low, 5:6], 0.0)
     denom = near0 + far0 + jnp.concatenate([near_a + far_a, near_b + far_b], axis=0)
-
-    qs.ring_recv(0)
-    ws.begin()
 
     def flat(lo, hi, a, b):
         return posr[lo:hi, a:b].reshape((hi - lo) * (b - a), width)
@@ -294,24 +327,31 @@
 
     for item in locals_[6:]:
         item.wait()
-    qs.own_recv()
+    for part in parts:
+        part.own_recv()
     multiply(r, True)
 
     for step in range(1, half):
         last = step == half - 1
         if not last:
-            qs.ring_recv(step)
-        qs.y_recv(step - 1)
-        qs.core_recv(step - 1)
+            for part in parts:
+                part.ring_recv(step)
+        for part in parts:
+            part.y_recv(step - 1)
+        for part in parts:
+            part.core_recv(step - 1)
         multiply(row_at(p - step))
         multiply(row_at(p + step))
         if last:
-            qs.ring_recv(step)
+            for part in parts:
+                part.ring_recv(step)
         ws.ring_recv(step - 1)
         if step >= 2:
             ws.y_recv(step - 2)
-    qs.y_recv(half - 1)
-    qs.core_recv(half - 1)
+    for part in parts:
+        part.y_recv(half - 1)
+    for part in parts:
+        part.core_recv(half - 1)
     multiply(row_at(p + half))
 
     def attend(h):
@@ -339,48 +379,59 @@
 
     merged = att[...].astype(jnp.bfloat16).astype(jnp.float32) * wcol[:, 1:2]
     merged = merged.reshape(win, win, hd)
-    rim_out[...] = merged[:, tile:].reshape(win * tile, hd).astype(jnp.bfloat16)
-    start("rc", rim_out, rim_in, to_core)
-    own = merged[:, :tile].reshape(win * tile, hd)
+    near_out[...] = merged[:, :tile].reshape(win * tile, hd).astype(jnp.bfloat16)
+    far_out[...] = merged[:, tile:].reshape(win * tile, hd).astype(jnp.bfloat16)
+    top, mid, bottom = pl.ds(0, low), pl.ds(low, high - low), pl.ds(high, low)
+    send_up = [copy("rt", near_out.at[top], near_in.at[bottom], (g, above, c)),
+               copy("st", far_out.at[top], far_in.at[bottom], (g, above, other))]
+    send_down = [copy("rb", near_out.at[bottom], near_in.at[top], (g, below, c)),
+                 copy("sb", far_out.at[bottom], far_in.at[top], (g, below, other))]
+
+    @pl.when(has_above)
+    def _():
+        for item in send_up:
+            item.start()
+
+    @pl.when(has_below)
+    def _():
+        for item in send_down:
+            item.start()
+
+    start("rc", far_out.at[mid], far_in.at[mid], to_core)
+    own = merged[:, :tile].reshape(win * tile, hd)[low:high]
+
+    @pl.when(r == 0)
+    def _():
+        near_in[0:low] = jnp.zeros((low, hd), near_in.dtype)
+        far_in[0:low] = jnp.zeros((low, hd), far_in.dtype)
+
+    @pl.when(r == rows - 1)
+    def _():
+        near_in[high:] = jnp.zeros((low, hd), near_in.dtype)
+        far_in[high:] = jnp.zeros((low, hd), far_in.dtype)
+
     ws.y_recv(half - 1)
-    arrived("rc", rim_in)
-    own = own + jnp.where(fold_ok, rim_in[...].astype(jnp.float32), 0.0)
-    top_out[...] = own[:low].astype(jnp.bfloat16)
-    bot_out[...] = own[high:].astype(jnp.bfloat16)
-    send_top = copy("rt", top_out, bot_in, (g, above, c))
-    send_bot = copy("rb", bot_out, top_in, (g, below, c))
-
-    @pl.when(r > 0)
-    def _():
-        send_top.start()
-
-    @pl.when(r < rows - 1)
-    def _():
-        send_bot.start()
-
-    @pl.when(r == 0)
-    def _():
-        top_in[...] = jnp.zeros_like(top_in)
-
-    @pl.when(r == rows - 1)
-    def _():
-        bot_in[...] = jnp.zeros_like(bot_in)
-
     for step in range(half):
         ws.core_recv(step)
     ws.own_recv()
-
-    @pl.when(r > 0)
-    def _():
-        send_bot.wait_recv()
-
-    @pl.when(r < rows - 1)
-    def _():
-        send_top.wait_recv()
-
-    own = own[low:high] + jnp.concatenate(
-        [top_in[...].astype(jnp.float32), bot_in[...].astype(jnp.float32)], axis=0
-    )
+    arrived("rc", far_in.at[mid])
+
+    @pl.when(has_above)
+    def _():
+        for item in send_down:
+            item.wait_recv()
+
+    @pl.when(has_below)
+    def _():
+        for item in send_up:
+            item.wait_recv()
+
+    far_got = jnp.where(fold_ok, far_in[...].astype(jnp.float32), 0.0)
+    edge = jnp.concatenate(
+        [near_in[0:low].astype(jnp.float32) + far_got[:low],
+         near_in[high:].astype(jnp.float32) + far_got[high:]], axis=0
+    )
+    own = own + far_got[low:high] + edge
     result = base[...] + lax.dot_general(
         own.astype(jnp.bfloat16), wo_all[...].reshape(width, hd),
         (((1,), (1,)), ((), ())), preferred_element_type=jnp.float32,
@@ -391,17 +442,15 @@
     for item in pending:
         item.wait_send()
 
-    @pl.when(r > 0)
-    def _():
-        halo_up.wait_send()
-        fwd_top.wait_send()
-        send_top.wait_send()
-
-    @pl.when(r < rows - 1)
-    def _():
-        halo_down.wait_send()
-        fwd_bot.wait_send()
-        send_bot.wait_send()
+    @pl.when(has_above)
+    def _():
+        for item in [halo_up, fwd_top] + count_up + send_up:
+            item.wait_send()
+
+    @pl.when(has_below)
+    def _():
+        for item in [halo_down, fwd_bot] + count_down + send_down:
+            item.wait_send()
 
 
 def fused(rows, embeddings, pos_embed, ln_gain, ln_bias, w_qkv, b_qkv, w_out, b_out, valid):
@@ -410,7 +459,6 @@
     tok = win * win
     shard, qkv = w_qkv.shape
     hd = w_out.shape[1]
-    copies = 8 * 8 * rows
     bf16, f32 = jnp.bfloat16, jnp.float32
     vmem = pl.BlockSpec(memory_space=pltpu.VMEM)
     return pl.pallas_call(
@@ -436,12 +484,10 @@
             pltpu.VMEM((tok, hd), f32),
             pltpu.VMEM((win * tile, hd), bf16),
             pltpu.VMEM((win * tile, hd), bf16),
-            pltpu.VMEM((rim * tile, hd), bf16),
-            pltpu.VMEM((rim * tile, hd), bf16),
-            pltpu.VMEM((rim * tile, hd), bf16),
-            pltpu.VMEM((rim * tile, hd), bf16),
-            pltpu.SemaphoreType.DMA((96,)),
-            pltpu.SemaphoreType.DMA((96,)),
+            pltpu.VMEM((win * tile, hd), bf16),
+            pltpu.VMEM((win * tile, hd), bf16),
+            pltpu.SemaphoreType.DMA((16 + 20 * rows,)),
+            pltpu.SemaphoreType.DMA((16 + 20 * rows,)),
             pltpu.SemaphoreType.DMA((9,)),
         ],
         compiler_params=pltpu.CompilerParams(

time: 50 us -> 47.4 us (0.948); the launches traced: 49.8 us -> 46.6 us
  Pallas kernels: 48.2 us -> 45 us
    pallas_call x1, Pallas kernels: 48.2 us -> 45 us  [fused(): pl.pallas_call(functools.partial(kernel, rows), out_shape=jax.ShapeDtypeS...]
where the time goes in v3:
time: 47.4 us; the launch traced here: 46.6 us
  Pallas kernels  45 us (95%)
  local copies, waits for them, and re-layouts  1.59 us (3%)
    pallas_call x1, Pallas kernels, fused(): pl.pallas_call(functools.partial(kernel, rows), out_shape=jax.ShapeDtypeS...  45 us
    unnamed x1, local copies, waits for them, and re-layouts  1.59 us

profile of v3, /device:TPU:0, one launch (start us, length us, event | category | flops | bytes accessed | tf_op | source)
XLA Modules:
  0.0 46.6 jit_solution(12276548348781020803)
XLA Ops:
  0.0 45.0 %shard_map.91 = bf16[8,8,1280]{2,1,0:T(8,128)(2,1)} custom-call(bf16[8,8,1280]{2,1,0:T(8,128)(2,1)} %emb_ref.1, bf16[256,1280]{1,0:T(8,128)(2,1)} %pos_hbm.1, f32[1280]{0:T(1024)} %gain_hbm.1, f32[1280]{0:T(1024)} %bias_hbm.1, bf16[80,1920]{1,0:T(8,128)(2,1)} %wq_ref.1, f32[1920]{0:T(1024)} %bq_hbm.1, bf16[80,640]{1,0:T(8,128)(2,1)} %wo_ref.1, f32[1280]{0:T(1024)} %bo_hbm.1, ...), custom_call_target="tpu_custom_call" | custom-call | tf_op jit(solution)/shard_map/pallas_call | solution.py:464
  45.0 1.6 %copy.11 = bf16[8,8,1280]{2,1,0:T(8,128)(2,1)} copy(bf16[8,8,1280]{2,1,0:T(8,128)(2,1)} %shard_map.91) | data formatting | bytes 327680

commit v4 on v3

--- a/solution.py
+++ b/solution.py
@@ -331,23 +331,32 @@
         part.own_recv()
     multiply(r, True)
 
-    for step in range(1, half):
-        last = step == half - 1
-        if not last:
-            for part in parts:
-                part.ring_recv(step)
+    early_part, late_part = parts
+    for step in range(1, half - 1):
+        early_part.ring_recv(step)
+        if step > 1:
+            multiply(row_at(p + step - 1))
+        late_part.ring_recv(step)
         for part in parts:
             part.y_recv(step - 1)
+        ws.ring_recv(step - 1)
         for part in parts:
             part.core_recv(step - 1)
         multiply(row_at(p - step))
-        multiply(row_at(p + step))
-        if last:
-            for part in parts:
-                part.ring_recv(step)
-        ws.ring_recv(step - 1)
         if step >= 2:
             ws.y_recv(step - 2)
+    for part in parts:
+        part.y_recv(half - 2)
+    multiply(row_at(p + half - 2))
+    ws.ring_recv(half - 2)
+    ws.y_recv(half - 3)
+    for part in parts:
+        part.ring_recv(half - 1)
+    for part in parts:
+        part.core_recv(half - 2)
+    multiply(row_at(p - half + 1))
+    multiply(row_at(p + half - 1))
+    ws.y_recv(half - 2)
     for part in parts:
         part.y_recv(half - 1)
     for part in parts:
@@ -372,10 +381,9 @@
 
     for h in range(HEADS // 2):
         attend(h)
-    ws.y_recv(half - 2)
+    ws.ring_recv(half - 1)
     for h in range(HEADS // 2, HEADS):
         attend(h)
-    ws.ring_recv(half - 1)
 
     merged = att[...].astype(jnp.bfloat16).astype(jnp.float32) * wcol[:, 1:2]
     merged = merged.reshape(win, win, hd)

time: 47.4 us -> 46.5 us (0.981)
  the two profiles are of different devices: /device:TPU:0 before, /device:TPU:10 now
where the time goes in v4:
time: 46.5 us; the launch traced here: 46.4 us
  Pallas kernels  44.8 us (96%)
  local copies, waits for them, and re-layouts  1.59 us (3%)
    pallas_call x1, Pallas kernels, fused(): pl.pallas_call(functools.partial(kernel, rows), out_shape=jax.ShapeDtypeS...  44.8 us
    unnamed x1, local copies, waits for them, and re-layouts  1.59 us

profile of v4, /device:TPU:10, one launch (start us, length us, event | category | flops | bytes accessed | tf_op | source)
XLA Modules:
  0.0 46.4 jit_solution(6406083610693653977)
XLA Ops:
  0.0 44.8 %shard_map.91 = bf16[8,8,1280]{2,1,0:T(8,128)(2,1)} custom-call(bf16[8,8,1280]{2,1,0:T(8,128)(2,1)} %emb_ref.1, bf16[256,1280]{1,0:T(8,128)(2,1)} %pos_hbm.1, f32[1280]{0:T(1024)} %gain_hbm.1, f32[1280]{0:T(1024)} %bias_hbm.1, bf16[80,1920]{1,0:T(8,128)(2,1)} %wq_ref.1, f32[1920]{0:T(1024)} %bq_hbm.1, bf16[80,640]{1,0:T(8,128)(2,1)} %wo_ref.1, f32[1280]{0:T(1024)} %bo_hbm.1, ...), custom_call_target="tpu_custom_call" | custom-call | tf_op jit(solution)/shard_map/pallas_call | solution.py:472
  44.8 1.6 %copy.11 = bf16[8,8,1280]{2,1,0:T(8,128)(2,1)} copy(bf16[8,8,1280]{2,1,0:T(8,128)(2,1)} %shard_map.91) | data formatting | bytes 327680

commit v5 on v4

--- a/solution.py
+++ b/solution.py
@@ -76,7 +76,7 @@
 
     barrier = pltpu.get_barrier_semaphore()
     has_above, has_below = r > 0, r < rows - 1
-    for peer in (to_core, to_y, (g, ahead, c), (g, behind, c)):
+    for peer in (to_core, to_y, (g, ahead, c), (g, behind, c), (g, ahead, other)):
         pl.semaphore_signal(barrier, inc=1, device_id=peer, device_id_type=MESH)
 
     @pl.when(has_above)
@@ -89,7 +89,7 @@
         for core in (c, other):
             pl.semaphore_signal(barrier, inc=1, device_id=(g, below, core), device_id_type=MESH)
 
-    pl.semaphore_wait(barrier, 8 - 2 * (r == 0).astype(jnp.int32) - 2 * (r == rows - 1).astype(jnp.int32))
+    pl.semaphore_wait(barrier, 9 - 2 * (r == 0).astype(jnp.int32) - 2 * (r == rows - 1).astype(jnp.int32))
 
     halo_down = copy("hd", emb_ref.at[pl.ds(tile - rim, rim)], eb.at[0, pl.ds(0, rim)], (g, below, c))
     halo_up = copy("hu", emb_ref.at[pl.ds(0, rim)], eb.at[0, pl.ds(rim + tile, rim)], (g, above, c))
@@ -164,9 +164,11 @@
                     arrived(f"{self.name}y{way}{step}", here)
                     if step == half - 2 and way == 0:
                         start(f"{self.name}l", here, here, (g, ahead, c))
+                        start(f"{self.name}d{way}{half - 1}", here, here, (g, ahead, other))
                 else:
                     arrived(f"{self.name}l", here)
-                start(f"{self.name}d{way}{step}", here, here, to_core)
+                if step < half - 1:
+                    start(f"{self.name}d{way}{step}", here, here, to_core)
 
         def core_recv(self, step):
             for way in self.ways(step):

time: 46.5 us -> 44.9 us (0.966)
  the two profiles are of different devices: /device:TPU:10 before, /device:TPU:0 now
where the time goes in v5:
time: 44.9 us; the launch traced here: 44.2 us
  Pallas kernels  42.6 us (95%)
  local copies, waits for them, and re-layouts  1.59 us (4%)
    pallas_call x1, Pallas kernels, fused(): pl.pallas_call(functools.partial(kernel, rows), out_shape=jax.ShapeDtypeS...  42.6 us
    unnamed x1, local copies, waits for them, and re-layouts  1.59 us

profile of v5, /device:TPU:0, one launch (start us, length us, event | category | flops | bytes accessed | tf_op | source)
XLA Modules:
  0.0 44.2 jit_solution(16952559902388227390)
XLA Ops:
  0.0 42.6 %shard_map.91 = bf16[8,8,1280]{2,1,0:T(8,128)(2,1)} custom-call(bf16[8,8,1280]{2,1,0:T(8,128)(2,1)} %emb_ref.1, bf16[256,1280]{1,0:T(8,128)(2,1)} %pos_hbm.1, f32[1280]{0:T(1024)} %gain_hbm.1, f32[1280]{0:T(1024)} %bias_hbm.1, bf16[80,1920]{1,0:T(8,128)(2,1)} %wq_ref.1, f32[1920]{0:T(1024)} %bq_hbm.1, bf16[80,640]{1,0:T(8,128)(2,1)} %wo_ref.1, f32[1280]{0:T(1024)} %bo_hbm.1, ...), custom_call_target="tpu_custom_call" | custom-call | tf_op jit(solution)/shard_map/pallas_call | solution.py:474
  42.6 1.6 %copy.11 = bf16[8,8,1280]{2,1,0:T(8,128)(2,1)} copy(bf16[8,8,1280]{2,1,0:T(8,128)(2,1)} %shard_map.91) | data formatting | bytes 327680
